TPU v7x, 32 devices: a whole 2x2x4 slice. The times are simulated.
32 devices in a mesh: dp: 8 (over z, x), comp: 4 (over y, core).
Axes of the slice: x: 2, y: 2, z: 4, core: 2. Of those that a mesh axis runs over, the one named last changes fastest.
Arguments:
- points: float32 [1024, 1024], P('dp'), may hold values from -4.25 to 4.25
- centres: float32 [4096, 1024], P('comp'), may hold values from -1 to 1
- variances: float32 [4096, 1024], P('comp'), may hold values from 0.15 to 2
- mix_logits: float32 [4096], P('comp'), may hold values from -2 to 2
Outputs:
- new_centres: float32 [4096, 1024], P('comp')
- new_variances: float32 [4096, 1024], P('comp')
- log_weights: float32 [4096], P('comp')
- log_likelihood: float32 [1024], P('dp')
All inputs are finite; a program needn't handle non-finite values.
Results may differ from a plain program's by a relative error of at most 0.0014.
Values sent between devices are 32-bit elements; how exact they have to be, the bound alone decides.
A program may use at most 128 MiB of HBM per device.

v0:
```python
import functools
import math

import jax
import jax.numpy as jnp
from jax import lax
from jax.experimental import pallas as pl
from jax.experimental.pallas import tpu as pltpu
from jax.sharding import PartitionSpec as P

ITERS = 2

LOG_TWO_PI = math.log(2.0 * math.pi)

VMEM_BYTES = 60 * 2**20
TILE = 256


def dot(left, right, contract):
    return lax.dot_general(
        left,
        right,
        (contract, ((), ())),
        precision=lax.Precision.HIGH,
        preferred_element_type=jnp.float32,
    )


def on_device(points, centres, variances, mix_logits):
    width = points.shape[1]
    every = lax.all_gather(points, "dp", axis=0, tiled=True)
    both = jnp.concatenate([every * every, every], 1)
    mine = lax.axis_index("dp") * points.shape[0]
    total = jnp.float32(every.shape[0] + centres.shape[0] * lax.axis_size("comp"))
    log_norm = None
    for iteration in range(ITERS):
        inverse = 1.0 / variances
        scaled = centres * inverse
        offset = jnp.sum(centres * scaled, 1) + jnp.sum(jnp.log(variances), 1) + width * LOG_TWO_PI
        quadratic = dot(jnp.concatenate([inverse, -2.0 * scaled], 1), both, ((1,), (1,)))
        density = (mix_logits - 0.5 * offset)[:, None] - 0.5 * quadratic
        highest = jnp.max(density, 0)
        summed = jnp.sum(jnp.exp(density - highest[None, :]), 0)
        parts = lax.all_gather(jnp.stack([highest, summed]), "comp", axis=0)
        peak = jnp.max(parts[:, 0], 0)
        log_norm = peak + jnp.log(jnp.sum(parts[:, 1] * jnp.exp(parts[:, 0] - peak), 0))
        shares = jnp.exp(density - log_norm[None, :])
        counts = jnp.sum(shares, 1)
        moments = dot(shares, both, ((1,), (0,)))
        second, first = moments[:, :width], moments[:, width:]
        plus_one = (counts + 1.0)[:, None]
        centres = first / plus_one
        variances = (second - 2.0 * centres * first + plus_one * centres * centres + 1.0) / (
            counts + 2.0
        )[:, None]
        mix_logits = jnp.log((counts + 1.0) / total)
    log_norm = lax.dynamic_slice_in_dim(log_norm, mine, points.shape[0], 0)
    return (centres, variances, mix_logits, log_norm)


def split(value):
    high = value.astype(jnp.bfloat16)
    return high, (value - high.astype(jnp.float32)).astype(jnp.bfloat16)


def mm(left, right, contract):
    return lax.dot_general(
        left, right, (contract, ((), ())), preferred_element_type=jnp.float32
    )


NT = ((1,), (1,))
NN = ((1,), (0,))


def shares_of(density, log_norm, rows):
    groups = density.shape[0]
    return jnp.concatenate(
        [jnp.exp(density[g, rows, :] - log_norm[g]) for g in range(groups)], 1
    )


def m_step(shares, right_high, right_low, cols, width, counts):
    high, low = split(shares)

    def moment(at):
        rh = right_high[:, at]
        return mm(high, rh, NN) + (mm(high, right_low[:, at], NN) + mm(low, rh, NN))

    second = moment(pl.ds(cols.start, cols.size))
    first = moment(pl.ds(width + cols.start, cols.size))
    plus_one = counts + 1.0
    centre = first / plus_one
    var = (second - 2.0 * centre * first + plus_one * centre * centre + 1.0) / (counts + 2.0)
    return centre, var


CHUNK = 256


def left_of(centre, var, rows, start, width, left_high, left_low):
    inverse = 1.0 / var
    scaled = centre * inverse
    size = centre.shape[1]
    h, l = split(inverse)
    left_high[rows, pl.ds(start, size)] = h
    left_low[rows, pl.ds(start, size)] = l
    h, l = split(-2.0 * scaled)
    left_high[rows, pl.ds(width + start, size)] = h
    left_low[rows, pl.ds(width + start, size)] = l
    return jnp.sum(centre * scaled + jnp.log(var), 1, keepdims=True)


def em_kernel(
    dp,
    comp,
    points,
    centres_hbm,
    variances_hbm,
    logits,
    density_out,
    right_high_out,
    right_low_out,
    norm_out,
    buf,
    cbuf,
    vbuf,
    left_high,
    left_low,
    right_high,
    right_low,
    density,
    base,
    norm,
    stats,
    local_sem,
    sems,
    stat_sem,
):
    me = lax.axis_index("dp")
    ce = lax.axis_index("comp")
    groups = dp // 2
    z, x = me // 2, me % 2
    half = ce % 2
    rows_here, width = points.shape
    comps = cbuf.shape[0]
    pair = 2 * rows_here
    total = jnp.float32(dp * rows_here + comps * comp)
    mine = pl.ds(pl.multiple_of(half * (width // 2), 128), width // 2)
    other = pl.ds(pl.multiple_of((1 - half) * (width // 2), 128), width // 2)
    partner = {"dp": me, "comp": ce + 1 - 2 * half}
    across = {"dp": me + 1 - 2 * x, "comp": ce}

    loads = [
        pltpu.make_async_copy(points, buf.at[z, pl.ds(x * rows_here, rows_here)], local_sem.at[0]),
        pltpu.make_async_copy(variances_hbm, vbuf, local_sem.at[1]),
        pltpu.make_async_copy(centres_hbm, cbuf, local_sem.at[2]),
    ]
    for load in loads:
        load.start()

    barrier = pltpu.get_barrier_semaphore()
    for hop in range(1, comp):
        pl.semaphore_signal(
            barrier, inc=1, device_id={"dp": me, "comp": lax.rem(ce + hop, comp)}
        )
    pl.semaphore_signal(barrier, inc=1, device_id=across)

    if groups > 1:
        for step in (2, dp - 2):
            pl.semaphore_signal(
                barrier, inc=1, device_id={"dp": lax.rem(me + step, dp), "comp": ce}
            )
    pl.semaphore_wait(barrier, comp + (2 if groups > 1 else 0))

    def copy(block, cols, send, recv, device):
        at = buf.at[block // 2, pl.ds((block % 2) * rows_here, rows_here), cols]
        return pltpu.make_async_remote_copy(
            src_ref=at,
            dst_ref=at,
            send_sem=sems.at[send, block],
            recv_sem=sems.at[recv, block],
            device_id=device,
            device_id_type=pl.DeviceIdType.MESH,
        )

    def up(block):
        return copy(block, mine, 0, 4, {"dp": lax.rem(me + 2, dp), "comp": ce})

    def down(block):
        return copy(block, mine, 1, 4, {"dp": lax.rem(me + dp - 2, dp), "comp": ce})

    def cross(block):
        return copy(block, mine, 2, 5, across)

    def core(block):
        return copy(block, mine, 3, 6, partner)

    def core_in(block):
        return copy(block, other, 3, 6, partner)

    loads[0].wait()

    @pl.when(z < groups - 1)
    def _():
        up(me).start()

    @pl.when(z > 0)
    def _():
        down(me).start()

    cross(me).start()

    loads[1].wait()
    loads[2].wait()

    def prepare(t, carry):
        rows = pl.ds(pl.multiple_of(t * TILE, TILE), TILE)
        offset = jnp.zeros((TILE, 1), jnp.float32)
        for c in range(width // CHUNK):
            at = pl.ds(c * CHUNK, CHUNK)
            offset += left_of(
                cbuf[rows, at], vbuf[rows, at], rows, c * CHUNK, width, left_high, left_low
            )
        base[rows, :] = logits[rows, :] - 0.5 * (offset + width * LOG_TWO_PI)
        return carry

    lax.fori_loop(0, comps // TILE, prepare, 0)

    def e_tile(g, t):
        rows = pl.ds(pl.multiple_of(t * TILE, TILE), TILE)
        ns = pl.ds(pl.multiple_of(g * pair, pair), pair)
        lh, ll = left_high[rows, :], left_low[rows, :]
        rh, rl = right_high[ns, :], right_low[ns, :]
        quadratic = mm(lh, rh, NT) + (mm(lh, rl, NT) + mm(ll, rh, NT))
        density[g, rows, :] = base[rows, :] - 0.5 * quadratic

    def stat(turn, g):
        values = density[g]
        peak = jnp.max(values, 0, keepdims=True)
        stats[turn, ce, g, 0:1, :] = peak
        stats[turn, ce, g, 1:2, :] = jnp.sum(jnp.exp(values - peak), 0, keepdims=True)

    def compute(g):
        ns = pl.ds(pl.multiple_of(g * pair, pair), pair)
        for c in range(width // CHUNK):
            value = buf[g, :, pl.ds(c * CHUNK, CHUNK)]
            h, l = split(value * value)
            right_high[ns, pl.ds(c * CHUNK, CHUNK)] = h
            right_low[ns, pl.ds(c * CHUNK, CHUNK)] = l
            h, l = split(value)
            right_high[ns, pl.ds(width + c * CHUNK, CHUNK)] = h
            right_low[ns, pl.ds(width + c * CHUNK, CHUNK)] = l

        def tile(t, carry):
            e_tile(g, t)
            return carry

        lax.fori_loop(0, comps // TILE, tile, 0)
        stat(0, g)

    def ring(r, carry):
        @pl.when(jnp.logical_and(r > 0, z - r >= 0))
        def _():
            block = me - 2 * r
            up(block).wait_recv()

            @pl.when(z < groups - 1)
            def _():
                up(block).start()

            cross(block).start()
            core(block).start()

        @pl.when(jnp.logical_and(r > 0, z + r < groups))
        def _():
            block = me + 2 * r
            down(block).wait_recv()

            @pl.when(z > 0)
            def _():
                down(block).start()

            cross(block).start()
            core(block).start()

        def side(s, carry):
            g = z + (2 * s - 1) * (r - 1)
            present = jnp.logical_and(
                jnp.logical_and(g >= 0, g < groups),
                jnp.logical_and(r >= 1, jnp.logical_or(s == 0, r > 1)),
            )

            @pl.when(present)
            def _():
                block = 2 * g + 1 - x
                cross(block).wait_recv()
                core(block).start()

            return carry

        lax.fori_loop(0, 2, side, 0)

        def work(s, carry):
            g = z + (2 * s - 1) * (r - 2)
            present = jnp.logical_and(
                jnp.logical_and(g >= 0, g < groups),
                jnp.logical_and(r >= 2, jnp.logical_or(s == 0, r > 2)),
            )

            @pl.when(present)
            def _():
                @pl.when(r > 2)
                def _():
                    core_in(2 * g + x).wait_recv()

                core_in(2 * g + 1 - x).wait_recv()
                compute(g)

            return carry

        lax.fori_loop(0, 2, work, 0)
        return carry

    lax.fori_loop(0, groups + 2, ring, 0)

    def exchange(turn):
        def to(hop):
            return pltpu.make_async_remote_copy(
                src_ref=stats.at[turn, ce],
                dst_ref=stats.at[turn, ce],
                send_sem=stat_sem.at[turn, 0, hop - 1],
                recv_sem=stat_sem.at[turn, 1, hop - 1],
                device_id={"dp": me, "comp": lax.rem(ce + hop, comp)},
                device_id_type=pl.DeviceIdType.MESH,
            )

        for hop in range(1, comp):
            to(hop).start()
        for hop in range(1, comp):
            to(hop).wait()
        peak = stats[turn, 0, :, 0:1, :]
        for c in range(1, comp):
            peak = jnp.maximum(peak, stats[turn, c, :, 0:1, :])
        summed = jnp.zeros_like(peak)
        for c in range(comp):
            summed += stats[turn, c, :, 1:2, :] * jnp.exp(stats[turn, c, :, 0:1, :] - peak)
        norm[...] = peak + jnp.log(summed)

    exchange(0)

    outs = [
        pltpu.make_async_copy(right_high, right_high_out, local_sem.at[0]),
        pltpu.make_async_copy(right_low, right_low_out, local_sem.at[1]),
    ]
    for out in outs:
        out.start()

    def again(t, carry):
        rows = pl.ds(pl.multiple_of(t * TILE, TILE), TILE)
        shares = shares_of(density, norm, rows)
        counts = jnp.sum(shares, 1, keepdims=True)
        offset = jnp.zeros((TILE, 1), jnp.float32)
        for c in range(width // CHUNK):
            centre, var = m_step(
                shares, right_high, right_low, pl.ds(c * CHUNK, CHUNK), width, counts
            )
            offset += left_of(centre, var, rows, c * CHUNK, width, left_high, left_low)
        logit = jnp.log((counts + 1.0) / total)
        base[rows, :] = logit - 0.5 * (offset + width * LOG_TWO_PI)

        def group(g, carry):
            e_tile(g, t)
            return carry

        lax.fori_loop(0, groups, group, 0)
        return carry

    for turn in range(1, ITERS):
        lax.fori_loop(0, comps // TILE, again, 0)

        def each(g, carry, turn=turn):
            stat(turn, g)
            return carry

        lax.fori_loop(0, groups, each, 0)
        exchange(turn)

    last = pltpu.make_async_copy(density, density_out, local_sem.at[2])
    last.start()
    norm_out[...] = norm[...]

    @pl.when(z < groups - 1)
    def _():
        up(me).wait_send()

    @pl.when(z > 0)
    def _():
        down(me).wait_send()

    cross(me).wait_send()

    def drain(block, carry):
        g = block // 2

        @pl.when(jnp.logical_and(block % 2 == x, g < z))
        def _():
            @pl.when(z < groups - 1)
            def _():
                up(block).wait_send()

            cross(block).wait_send()

        @pl.when(jnp.logical_and(block % 2 == x, g > z))
        def _():
            @pl.when(z > 0)
            def _():
                down(block).wait_send()

            cross(block).wait_send()

        @pl.when(block != me)
        def _():
            core(block).wait_send()

        return carry

    lax.fori_loop(0, dp, drain, 0)
    last.wait()
    for out in outs:
        out.wait()


def last_kernel(total, density, norm, right_high, right_low, centre_out, var_out, logit_out):
    width = centre_out.shape[1]
    shares = shares_of(density, norm, slice(None))
    counts = jnp.sum(shares, 1, keepdims=True)
    for c in range(width // CHUNK):
        at = pl.ds(c * CHUNK, CHUNK)
        centre, var = m_step(shares, right_high, right_low, at, width, counts)
        centre_out[:, at] = centre
        var_out[:, at] = var
    logit_out[...] = jnp.log((counts + 1.0) / total)


def fused(dp, comp, points, centres, variances, mix_logits):
    rows_here, width = points.shape
    comps = centres.shape[0]
    groups, pair, every = dp // 2, 2 * rows_here, dp * rows_here
    f32, bf16 = jnp.float32, jnp.bfloat16
    vmem, anyw = pl.BlockSpec(memory_space=pltpu.VMEM), pl.BlockSpec(memory_space=pl.ANY)
    density, high, low, norm = pl.pallas_call(
        functools.partial(em_kernel, dp, comp),
        out_shape=[
            jax.ShapeDtypeStruct((groups, comps, pair), f32),
            jax.ShapeDtypeStruct((every, 2 * width), bf16),
            jax.ShapeDtypeStruct((every, 2 * width), bf16),
            jax.ShapeDtypeStruct((groups, 1, pair), f32),
        ],
        in_specs=[anyw, anyw, anyw, vmem],
        out_specs=[anyw, anyw, anyw, vmem],
        scratch_shapes=[
            pltpu.VMEM((groups, pair, width), f32),
            pltpu.VMEM((comps, width), f32),
            pltpu.VMEM((comps, width), f32),
            pltpu.VMEM((comps, 2 * width), bf16),
            pltpu.VMEM((comps, 2 * width), bf16),
            pltpu.VMEM((every, 2 * width), bf16),
            pltpu.VMEM((every, 2 * width), bf16),
            pltpu.VMEM((groups, comps, pair), f32),
            pltpu.VMEM((comps, 1), f32),
            pltpu.VMEM((groups, 1, pair), f32),
            pltpu.VMEM((ITERS, comp, groups, 2, pair), f32),
            pltpu.SemaphoreType.DMA((3,)),
            pltpu.SemaphoreType.DMA((7, dp)),
            pltpu.SemaphoreType.DMA((ITERS, 2, comp - 1)),
        ],
        compiler_params=pltpu.CompilerParams(
            collective_id=0, has_side_effects=True, vmem_limit_bytes=VMEM_BYTES
        ),
        name="em",
    )(points, centres, variances, mix_logits[:, None])
    total = float(every + comps * comp)
    whole = lambda *shape: pl.BlockSpec(shape, lambda t: (0,) * len(shape))
    centre, var, logit = pl.pallas_call(
        functools.partial(last_kernel, total),
        grid=(comps // TILE,),
        out_shape=[
            jax.ShapeDtypeStruct((comps, width), f32),
            jax.ShapeDtypeStruct((comps, width), f32),
            jax.ShapeDtypeStruct((comps, 1), f32),
        ],
        in_specs=[
            pl.BlockSpec((groups, TILE, pair), lambda t: (0, t, 0)),
            whole(groups, 1, pair),
            whole(every, 2 * width),
            whole(every, 2 * width),
        ],
        out_specs=[
            pl.BlockSpec((TILE, width), lambda t: (t, 0)),
            pl.BlockSpec((TILE, width), lambda t: (t, 0)),
            pl.BlockSpec((TILE, 1), lambda t: (t, 0)),
        ],
        compiler_params=pltpu.CompilerParams(vmem_limit_bytes=VMEM_BYTES),
        name="last",
    )(density, norm, high, low)
    here = lax.axis_index("dp")
    log_norm = lax.dynamic_slice_in_dim(norm.reshape(every), here * rows_here, rows_here, 0)
    return centre, var, logit[:, 0], log_norm


def solution(mesh):
    dp, comp = mesh.shape["dp"], mesh.shape["comp"]

    def body(points, centres, variances, mix_logits):
        rows, width = points.shape
        comps = centres.shape[0]
        every = dp * rows
        need = every * width * 12 + comps * width * 16 + comps * every * 4
        fits = need < VMEM_BYTES * 3 // 4 and dp % 2 == 0 and comp % 2 == 0
        form = functools.partial(fused, dp, comp) if fits else on_device
        return form(points, centres, variances, mix_logits)

    return jax.shard_map(
        body,
        mesh=mesh,
        in_specs=(P("dp", None), P("comp", None), P("comp", None), P("comp")),
        out_specs=(P("comp", None), P("comp", None), P("comp"), P("dp")),
        check_vma=False,
    )
```

profile of v0, /device:TPU:13, one launch (start us, length us, event | category | flops | bytes accessed | tf_op | source)
XLA Modules:
  0.0 112.4 jit_solution(2792051350796020986)
XLA Ops:
  0.6 1.7 %copy.8.logits = f32[1024,1]{1,0:T(8,128)} copy(f32[1024,1]{0,1:T(1,128)} %bitcast.2) | data formatting | bytes 8192 | tf_op jit(solution)/shard_map/broadcast_in_dim | solution.py:482
  2.3 87.7 %em.1 = (f32[4,1024,256]{2,1,0:T(8,128)}, bf16[1024,2048]{1,0:T(8,128)(2,1)}, bf16[1024,2048]{1,0:T(8,128)(2,1)}, f32[4,1,256]{2,1,0:T(1,128)}) custom-call(f32[128,1024]{1,0:T(8,128)} %points.1, f32[1024,1024]{1,0:T(8,128)} %centres_hbm.1, f32[1024,1024]{1,0:T(8,128)} %variances_hbm.1, f32[1024,1]{1,0:T(8,128)} %copy.8.logits), custom_call_target="tpu_custom_call" | custom-call | tf_op jit(solution)/shard_map/em/pallas_call | solution.py:452
  90.0 19.3 %last.1 = (f32[1024,1024]{1,0:T(8,128)}, f32[1024,1024]{1,0:T(8,128)}, f32[1024,1]{1,0:T(8,128)}) custom-call(f32[4,1024,256]{2,1,0:T(8,128)} %get-tuple-element.11.density, f32[4,1,256]{2,1,0:T(1,128)} %get-tuple-element.12.norm, bf16[1024,2048]{1,0:T(8,128)(2,1)} %get-tuple-element.13.right_high, bf16[1024,2048]{1,0:T(8,128)(2,1)} %get-tuple-element.14.right_low), custom_call_target="tpu_custom_call" | custom-call | tf_op jit(solution)/shard_map/last/pallas_call | solution.py:485
  109.4 1.8 %reduce = f32[1024]{0:T(1024)} reduce(f32[1024,1]{1,0:T(8,128)} %get-tuple-element.17, f32[]{:T(128)} %constant.12), dimensions={1}, to_apply=%get-tuple-element.17.reduce_sub_computation | reduce | bytes 8196 | tf_op jit(solution)/shard_map/last/pallas_call | solution.py:485
  111.2 1.2 %dynamic_slice.3 = f32[128]{0:T(128)} dynamic-slice(f32[1024]{0:T(1024)} %bitcast.3, s32[]{:T(128)S(6)} %select_n.3), dynamic_slice_sizes={128} | dynamic-slice | bytes 1028 | tf_op jit(solution)/shard_map/dynamic_slice | solution.py:508
where the time goes:
time: 113 us; the launch traced here: 112 us
  Pallas kernels  107 us (95%)
  local copies, waits for them, and re-layouts  2.95 us (3%)
  other arithmetic  1.84 us (2%)
    pallas_call x1, Pallas kernels, fused(): pl.pallas_call(functools.partial(em_kernel, dp, comp), out_shape=[jax.Sha...  87.7 us
    pallas_call x1, Pallas kernels, fused(): pl.pallas_call(functools.partial(last_kernel, total), grid=(comps // TILE...  19.3 us

commit v1 on v0

--- a/solution.py
+++ b/solution.py
@@ -73,6 +73,36 @@
 NN = ((1,), (0,))
 
 
+LANES = 128
+
+
+def diagonal():
+    shape = (LANES, LANES)
+    return lax.broadcasted_iota(jnp.int32, shape, 0) == lax.broadcasted_iota(jnp.int32, shape, 1)
+
+
+def to_column(row):
+    keep = diagonal()
+    return jnp.concatenate(
+        [
+            jnp.sum(jnp.where(keep, row[:, c : c + LANES], 0.0), 1, keepdims=True)
+            for c in range(0, row.shape[1], LANES)
+        ],
+        0,
+    )
+
+
+def to_row(column):
+    keep = diagonal()
+    return jnp.concatenate(
+        [
+            jnp.sum(jnp.where(keep, column[c : c + LANES, :], 0.0), 0, keepdims=True)
+            for c in range(0, column.shape[0], LANES)
+        ],
+        1,
+    )
+
+
 def shares_of(density, log_norm, rows):
     groups = density.shape[0]
     return jnp.concatenate(
@@ -80,9 +110,7 @@
     )
 
 
-def m_step(shares, right_high, right_low, cols, width, counts):
-    high, low = split(shares)
-
+def m_step(high, low, right_high, right_low, cols, width, counts):
     def moment(at):
         rh = right_high[:, at]
         return mm(high, rh, NN) + (mm(high, right_low[:, at], NN) + mm(low, rh, NN))
@@ -122,6 +150,7 @@
     right_high_out,
     right_low_out,
     norm_out,
+    mine_out,
     buf,
     cbuf,
     vbuf,
@@ -136,6 +165,7 @@
     local_sem,
     sems,
     stat_sem,
+    leave_sem,
 ):
     me = lax.axis_index("dp")
     ce = lax.axis_index("comp")
@@ -222,7 +252,7 @@
             offset += left_of(
                 cbuf[rows, at], vbuf[rows, at], rows, c * CHUNK, width, left_high, left_low
             )
-        base[rows, :] = logits[rows, :] - 0.5 * (offset + width * LOG_TWO_PI)
+        base[rows, :] = to_column(logits[:, rows]) - 0.5 * (offset + width * LOG_TWO_PI)
         return carry
 
     lax.fori_loop(0, comps // TILE, prepare, 0)
@@ -356,14 +386,21 @@
     for out in outs:
         out.start()
 
-    def again(t, carry):
+    def leave(t):
+        rows = pl.ds(pl.multiple_of(t * TILE, TILE), TILE)
+        return pltpu.make_async_copy(
+            density.at[:, rows, :], density_out.at[:, rows, :], leave_sem.at[t]
+        )
+
+    def again(turn, t, carry):
         rows = pl.ds(pl.multiple_of(t * TILE, TILE), TILE)
         shares = shares_of(density, norm, rows)
         counts = jnp.sum(shares, 1, keepdims=True)
+        high, low = split(shares)
         offset = jnp.zeros((TILE, 1), jnp.float32)
         for c in range(width // CHUNK):
             centre, var = m_step(
-                shares, right_high, right_low, pl.ds(c * CHUNK, CHUNK), width, counts
+                high, low, right_high, right_low, pl.ds(c * CHUNK, CHUNK), width, counts
             )
             offset += left_of(centre, var, rows, c * CHUNK, width, left_high, left_low)
         logit = jnp.log((counts + 1.0) / total)
@@ -374,10 +411,12 @@
             return carry
 
         lax.fori_loop(0, groups, group, 0)
+        if turn == ITERS - 1:
+            leave(t).start()
         return carry
 
     for turn in range(1, ITERS):
-        lax.fori_loop(0, comps // TILE, again, 0)
+        lax.fori_loop(0, comps // TILE, functools.partial(again, turn), 0)
 
         def each(g, carry, turn=turn):
             stat(turn, g)
@@ -386,9 +425,9 @@
         lax.fori_loop(0, groups, each, 0)
         exchange(turn)
 
-    last = pltpu.make_async_copy(density, density_out, local_sem.at[2])
-    last.start()
     norm_out[...] = norm[...]
+    lanes = pl.ds(pl.multiple_of(x * rows_here, LANES), rows_here)
+    mine_out[...] = norm[z, :, lanes]
 
     @pl.when(z < groups - 1)
     def _():
@@ -426,21 +465,39 @@
         return carry
 
     lax.fori_loop(0, dp, drain, 0)
-    last.wait()
+
+    def left(t, carry):
+        leave(t).wait()
+        return carry
+
+    lax.fori_loop(0, comps // TILE, left, 0)
     for out in outs:
         out.wait()
 
 
-def last_kernel(total, density, norm, right_high, right_low, centre_out, var_out, logit_out):
+def last_kernel(
+    total,
+    density,
+    norm,
+    right_high,
+    right_low,
+    mine,
+    centre_out,
+    var_out,
+    logit_out,
+    mine_out,
+):
     width = centre_out.shape[1]
     shares = shares_of(density, norm, slice(None))
     counts = jnp.sum(shares, 1, keepdims=True)
+    high, low = split(shares)
     for c in range(width // CHUNK):
         at = pl.ds(c * CHUNK, CHUNK)
-        centre, var = m_step(shares, right_high, right_low, at, width, counts)
+        centre, var = m_step(high, low, right_high, right_low, at, width, counts)
         centre_out[:, at] = centre
         var_out[:, at] = var
-    logit_out[...] = jnp.log((counts + 1.0) / total)
+    logit_out[...] = to_row(jnp.log((counts + 1.0) / total))
+    mine_out[...] = mine[...]
 
 
 def fused(dp, comp, points, centres, variances, mix_logits):
@@ -449,16 +506,17 @@
     groups, pair, every = dp // 2, 2 * rows_here, dp * rows_here
     f32, bf16 = jnp.float32, jnp.bfloat16
     vmem, anyw = pl.BlockSpec(memory_space=pltpu.VMEM), pl.BlockSpec(memory_space=pl.ANY)
-    density, high, low, norm = pl.pallas_call(
+    density, high, low, norm, mine = pl.pallas_call(
         functools.partial(em_kernel, dp, comp),
         out_shape=[
             jax.ShapeDtypeStruct((groups, comps, pair), f32),
             jax.ShapeDtypeStruct((every, 2 * width), bf16),
             jax.ShapeDtypeStruct((every, 2 * width), bf16),
             jax.ShapeDtypeStruct((groups, 1, pair), f32),
+            jax.ShapeDtypeStruct((1, rows_here), f32),
         ],
         in_specs=[anyw, anyw, anyw, vmem],
-        out_specs=[anyw, anyw, anyw, vmem],
+        out_specs=[anyw, anyw, anyw, vmem, vmem],
         scratch_shapes=[
             pltpu.VMEM((groups, pair, width), f32),
             pltpu.VMEM((comps, width), f32),
@@ -474,39 +532,41 @@
             pltpu.SemaphoreType.DMA((3,)),
             pltpu.SemaphoreType.DMA((7, dp)),
             pltpu.SemaphoreType.DMA((ITERS, 2, comp - 1)),
+            pltpu.SemaphoreType.DMA((comps // TILE,)),
         ],
         compiler_params=pltpu.CompilerParams(
             collective_id=0, has_side_effects=True, vmem_limit_bytes=VMEM_BYTES
         ),
         name="em",
-    )(points, centres, variances, mix_logits[:, None])
+    )(points, centres, variances, mix_logits[None, :])
     total = float(every + comps * comp)
     whole = lambda *shape: pl.BlockSpec(shape, lambda t: (0,) * len(shape))
-    centre, var, logit = pl.pallas_call(
+    centre, var, logit, log_norm = pl.pallas_call(
         functools.partial(last_kernel, total),
         grid=(comps // TILE,),
         out_shape=[
             jax.ShapeDtypeStruct((comps, width), f32),
             jax.ShapeDtypeStruct((comps, width), f32),
-            jax.ShapeDtypeStruct((comps, 1), f32),
+            jax.ShapeDtypeStruct((1, comps), f32),
+            jax.ShapeDtypeStruct((1, rows_here), f32),
         ],
         in_specs=[
             pl.BlockSpec((groups, TILE, pair), lambda t: (0, t, 0)),
             whole(groups, 1, pair),
             whole(every, 2 * width),
             whole(every, 2 * width),
+            whole(1, rows_here),
         ],
         out_specs=[
             pl.BlockSpec((TILE, width), lambda t: (t, 0)),
             pl.BlockSpec((TILE, width), lambda t: (t, 0)),
-            pl.BlockSpec((TILE, 1), lambda t: (t, 0)),
+            pl.BlockSpec((1, TILE), lambda t: (0, t)),
+            whole(1, rows_here),
         ],
         compiler_params=pltpu.CompilerParams(vmem_limit_bytes=VMEM_BYTES),
         name="last",
-    )(density, norm, high, low)
-    here = lax.axis_index("dp")
-    log_norm = lax.dynamic_slice_in_dim(norm.reshape(every), here * rows_here, rows_here, 0)
-    return centre, var, logit[:, 0], log_norm
+    )(density, norm, high, low, mine)
+    return centre, var, logit.reshape(comps), log_norm.reshape(rows_here)
 
 
 def solution(mesh):
@@ -518,6 +578,7 @@
         every = dp * rows
         need = every * width * 12 + comps * width * 16 + comps * every * 4
         fits = need < VMEM_BYTES * 3 // 4 and dp % 2 == 0 and comp % 2 == 0
+        fits = fits and rows % LANES == 0 and comps % TILE == 0
         form = functools.partial(fused, dp, comp) if fits else on_device
         return form(points, centres, variances, mix_logits)
 

time: 113 us -> 106 us (0.938)
  local copies, waits for them, and re-layouts: 2.95 us -> 0 us
  Pallas kernels: 107 us -> 105 us
  other arithmetic: 1.84 us -> 0 us
    pallas_call x1 -> x0, other arithmetic: 1.84 us -> none  [fused(): pl.pallas_call(functools.partial(last_kernel, total), grid=(comps // TILE...]
    pallas_call x1, Pallas kernels: 87.7 us -> 85.9 us  [fused(): pl.pallas_call(functools.partial(em_kernel, dp, comp), out_shape=[jax.Sha...]
    broadcast_in_dim x1 -> x0, local copies, waits for them, and re-layouts: 1.71 us -> none  [fused(): mix_logits[:, None]]
    dynamic_slice x1 -> x0, local copies, waits for them, and re-layouts: 1.25 us -> none  [fused(): lax.dynamic_slice_in_dim(norm.reshape(every), here * rows_here, rows_here...]
where the time goes in v1:
time: 106 us
  Pallas kernels  105 us (99%)
    pallas_call x1, Pallas kernels, fused(): pl.pallas_call(functools.partial(em_kernel, dp, comp), out_shape=[jax.Sha...  85.9 us
    pallas_call x1, Pallas kernels, fused(): pl.pallas_call(functools.partial(last_kernel, total), grid=(comps // TILE...  19.2 us

profile of v1, /device:TPU:13, one launch (start us, length us, event | category | flops | bytes accessed | tf_op | source)
XLA Modules:
  0.0 105.7 jit_solution(14084498265380043655)
XLA Ops:
  0.6 85.9 %em.1 = (f32[4,1024,256]{2,1,0:T(8,128)}, bf16[1024,2048]{1,0:T(8,128)(2,1)}, bf16[1024,2048]{1,0:T(8,128)(2,1)}, f32[4,1,256]{2,1,0:T(1,128)}, f32[1,128]{1,0:T(1,128)}) custom-call(f32[128,1024]{1,0:T(8,128)} %points.1, f32[1024,1024]{1,0:T(8,128)} %centres_hbm.1, f32[1024,1024]{1,0:T(8,128)} %variances_hbm.1, f32[1,1024]{1,0:T(1,128)} %bitcast.3), custom_call_target="tpu_custom_call" | custom-call | tf_op jit(solution)/shard_map/em/pallas_call | solution.py:509
  86.5 19.2 %last.1 = (f32[1024,1024]{1,0:T(8,128)}, f32[1024,1024]{1,0:T(8,128)}, f32[1,1024]{1,0:T(1,128)}, f32[1,128]{1,0:T(1,128)}) custom-call(f32[4,1024,256]{2,1,0:T(8,128)} %get-tuple-element.13.density, f32[4,1,256]{2,1,0:T(1,128)} %get-tuple-element.14.norm, bf16[1024,2048]{1,0:T(8,128)(2,1)} %get-tuple-element.15.right_high, ...), custom_call_target="tpu_custom_call" | custom-call | tf_op jit(solution)/shard_map/last/pallas_call | solution.py:544

commit v2 on v1

--- a/solution.py
+++ b/solution.py
@@ -176,9 +176,17 @@
     comps = cbuf.shape[0]
     pair = 2 * rows_here
     total = jnp.float32(dp * rows_here + comps * comp)
-    mine = pl.ds(pl.multiple_of(half * (width // 2), 128), width // 2)
-    other = pl.ds(pl.multiple_of((1 - half) * (width // 2), 128), width // 2)
+    y = (ce // 2) % 2
+
+    def cols_of(h, q, parts):
+        start = h * (width // 2) + q * (width // 4)
+        return pl.ds(pl.multiple_of(start, LANES), width // parts)
+
+    mine, other = cols_of(half, 0, 2), cols_of(1 - half, 0, 2)
+    mine_near, mine_far = cols_of(half, y, 4), cols_of(half, 1 - y, 4)
+    other_near, other_far = cols_of(1 - half, y, 4), cols_of(1 - half, 1 - y, 4)
     partner = {"dp": me, "comp": ce + 1 - 2 * half}
+    beside = {"dp": me, "comp": ce + 2 - 4 * y}
     across = {"dp": me + 1 - 2 * x, "comp": ce}
 
     loads = [
@@ -221,13 +229,16 @@
         return copy(block, mine, 1, 4, {"dp": lax.rem(me + dp - 2, dp), "comp": ce})
 
     def cross(block):
-        return copy(block, mine, 2, 5, across)
-
-    def core(block):
-        return copy(block, mine, 3, 6, partner)
-
-    def core_in(block):
-        return copy(block, other, 3, 6, partner)
+        return copy(block, mine_near, 2, 5, across)
+
+    def side(block, cols):
+        return copy(block, cols, 7, 8, beside)
+
+    def core(block, cols):
+        return copy(block, cols, 3, 6, partner)
+
+    def core_far(block, cols):
+        return copy(block, cols, 9, 10, partner)
 
     loads[0].wait()
 
@@ -240,9 +251,6 @@
         down(me).start()
 
     cross(me).start()
-
-    loads[1].wait()
-    loads[2].wait()
 
     def prepare(t, carry):
         rows = pl.ds(pl.multiple_of(t * TILE, TILE), TILE)
@@ -255,8 +263,6 @@
         base[rows, :] = to_column(logits[:, rows]) - 0.5 * (offset + width * LOG_TWO_PI)
         return carry
 
-    lax.fori_loop(0, comps // TILE, prepare, 0)
-
     def e_tile(g, t):
         rows = pl.ds(pl.multiple_of(t * TILE, TILE), TILE)
         ns = pl.ds(pl.multiple_of(g * pair, pair), pair)
@@ -289,8 +295,8 @@
         lax.fori_loop(0, comps // TILE, tile, 0)
         stat(0, g)
 
-    def ring(r, carry):
-        @pl.when(jnp.logical_and(r > 0, z - r >= 0))
+    def line(r):
+        @pl.when(z - r >= 0)
         def _():
             block = me - 2 * r
             up(block).wait_recv()
@@ -300,9 +306,9 @@
                 up(block).start()
 
             cross(block).start()
-            core(block).start()
-
-        @pl.when(jnp.logical_and(r > 0, z + r < groups))
+            core(block, mine).start()
+
+        @pl.when(z + r < groups)
         def _():
             block = me + 2 * r
             down(block).wait_recv()
@@ -312,44 +318,62 @@
                 down(block).start()
 
             cross(block).start()
-            core(block).start()
-
-        def side(s, carry):
-            g = z + (2 * s - 1) * (r - 1)
-            present = jnp.logical_and(
-                jnp.logical_and(g >= 0, g < groups),
-                jnp.logical_and(r >= 1, jnp.logical_or(s == 0, r > 1)),
-            )
-
-            @pl.when(present)
+            core(block, mine).start()
+
+    def each_at(distance, what):
+        def one(s, carry):
+            g = z + (2 * s - 1) * distance
+            inside = jnp.logical_and(g >= 0, g < groups)
+            fresh = jnp.logical_or(s == 0, distance > 0)
+
+            @pl.when(jnp.logical_and(distance >= 0, jnp.logical_and(inside, fresh)))
             def _():
-                block = 2 * g + 1 - x
-                cross(block).wait_recv()
-                core(block).start()
+                what(g)
 
             return carry
 
-        lax.fori_loop(0, 2, side, 0)
-
-        def work(s, carry):
-            g = z + (2 * s - 1) * (r - 2)
-            present = jnp.logical_and(
-                jnp.logical_and(g >= 0, g < groups),
-                jnp.logical_and(r >= 2, jnp.logical_or(s == 0, r > 2)),
-            )
-
-            @pl.when(present)
-            def _():
-                @pl.when(r > 2)
-                def _():
-                    core_in(2 * g + x).wait_recv()
-
-                core_in(2 * g + 1 - x).wait_recv()
-                compute(g)
-
-            return carry
-
-        lax.fori_loop(0, 2, work, 0)
+        lax.fori_loop(0, 2, one, 0)
+
+    def from_across(g):
+        block = 2 * g + 1 - x
+        cross(block).wait_recv()
+        side(block, mine_near).start()
+        core(block, mine_near).start()
+
+    def from_beside(g):
+        block = 2 * g + 1 - x
+        side(block, mine_far).wait_recv()
+        core_far(block, mine_far).start()
+
+    def work(g):
+        @pl.when(g != z)
+        def _():
+            core(2 * g + x, other).wait_recv()
+
+        core(2 * g + 1 - x, other_near).wait_recv()
+        core_far(2 * g + 1 - x, other_far).wait_recv()
+        compute(g)
+
+    def ring(r, carry):
+        @pl.when(jnp.logical_and(r > 0, r < groups - 1))
+        def _():
+            line(r)
+
+        each_at(r - 1, from_across)
+
+        @pl.when(r == 1)
+        def _():
+            loads[1].wait()
+            loads[2].wait()
+            lax.fori_loop(0, comps // TILE, prepare, 0)
+
+        each_at(r - 2, work)
+        each_at(r - 1, from_beside)
+
+        @pl.when(jnp.logical_and(r > 0, r == groups - 1))
+        def _():
+            line(r)
+
         return carry
 
     lax.fori_loop(0, groups + 2, ring, 0)
@@ -458,9 +482,15 @@
 
             cross(block).wait_send()
 
-        @pl.when(block != me)
-        def _():
-            core(block).wait_send()
+        @pl.when(jnp.logical_and(block % 2 == x, g != z))
+        def _():
+            core(block, mine).wait_send()
+
+        @pl.when(block % 2 != x)
+        def _():
+            side(block, mine_near).wait_send()
+            core(block, mine_near).wait_send()
+            core_far(block, mine_far).wait_send()
 
         return carry
 
@@ -530,7 +560,7 @@
             pltpu.VMEM((groups, 1, pair), f32),
             pltpu.VMEM((ITERS, comp, groups, 2, pair), f32),
             pltpu.SemaphoreType.DMA((3,)),
-            pltpu.SemaphoreType.DMA((7, dp)),
+            pltpu.SemaphoreType.DMA((11, dp)),
             pltpu.SemaphoreType.DMA((ITERS, 2, comp - 1)),
             pltpu.SemaphoreType.DMA((comps // TILE,)),
         ],
@@ -577,8 +607,8 @@
         comps = centres.shape[0]
         every = dp * rows
         need = every * width * 12 + comps * width * 16 + comps * every * 4
-        fits = need < VMEM_BYTES * 3 // 4 and dp % 2 == 0 and comp % 2 == 0
-        fits = fits and rows % LANES == 0 and comps % TILE == 0
+        fits = need < VMEM_BYTES * 3 // 4 and dp % 2 == 0 and comp % 4 == 0
+        fits = fits and rows % LANES == 0 and width % (4 * LANES) == 0 and comps % TILE == 0
         form = functools.partial(fused, dp, comp) if fits else on_device
         return form(points, centres, variances, mix_logits)
 

time: 106 us -> 107 us (level)
  the two profiles are of different devices: /device:TPU:13 before, /device:TPU:0 now
where the time goes in v2:
time: 107 us
  Pallas kernels  106 us (99%)
    pallas_call x1, Pallas kernels, fused(): pl.pallas_call(functools.partial(em_kernel, dp, comp), out_shape=[jax.Sha...  86.9 us
    pallas_call x1, Pallas kernels, fused(): pl.pallas_call(functools.partial(last_kernel, total), grid=(comps // TILE...  19.2 us

profile of v2, /device:TPU:0, one launch (start us, length us, event | category | flops | bytes accessed | tf_op | source)
XLA Modules:
  0.0 106.8 jit_solution(6027770266258407543)
XLA Ops:
  0.6 86.9 %em.1 = (f32[4,1024,256]{2,1,0:T(8,128)}, bf16[1024,2048]{1,0:T(8,128)(2,1)}, bf16[1024,2048]{1,0:T(8,128)(2,1)}, f32[4,1,256]{2,1,0:T(1,128)}, f32[1,128]{1,0:T(1,128)}) custom-call(f32[128,1024]{1,0:T(8,128)} %points.1, f32[1024,1024]{1,0:T(8,128)} %centres_hbm.1, f32[1024,1024]{1,0:T(8,128)} %variances_hbm.1, f32[1,1024]{1,0:T(1,128)} %bitcast.3), custom_call_target="tpu_custom_call" | custom-call | tf_op jit(solution)/shard_map/em/pallas_call | solution.py:539
  87.6 19.2 %last.1 = (f32[1024,1024]{1,0:T(8,128)}, f32[1024,1024]{1,0:T(8,128)}, f32[1,1024]{1,0:T(1,128)}, f32[1,128]{1,0:T(1,128)}) custom-call(f32[4,1024,256]{2,1,0:T(8,128)} %get-tuple-element.13.density, f32[4,1,256]{2,1,0:T(1,128)} %get-tuple-element.14.norm, bf16[1024,2048]{1,0:T(8,128)(2,1)} %get-tuple-element.15.right_high, ...), custom_call_target="tpu_custom_call" | custom-call | tf_op jit(solution)/shard_map/last/pallas_call | solution.py:574
